TPU v7x, 32 devices: a whole 2x2x4 slice. The times are simulated.
32 devices in a mesh: grp: 16 (over z, y, x), ep: 2 (over core).
Axes of the slice: x: 2, y: 2, z: 4, core: 2. Of those that a mesh axis runs over, the one named last changes fastest.
Arguments:
- tokens: bfloat16 [64, 7168], P(('grp', 'ep')), may hold values from -6 to 6
- expert_ids: int32 [64, 8], P(('grp', 'ep')), may hold values from 0 to 15, all different within a row; in each aligned block of 2 rows (0 to 1, 2 to 3, ...) at most 2 rows name the same one
- gate_ints: int32 [64, 8], P(('grp', 'ep')), may hold values from 1 to 16
- w_gate: bfloat16 [16, 7168, 2048], P('grp', None, 'ep'), may hold values from -0.0625 to 0.0625
- w_up: bfloat16 [16, 7168, 2048], P('grp', None, 'ep'), may hold values from -0.0625 to 0.0625
- w_down: bfloat16 [16, 2048, 7168], P('grp', 'ep'), may hold values from -0.125 to 0.125
Outputs:
- mixed: bfloat16 [64, 7168], P(('grp', 'ep'))
Inputs may be any that keep to these rules, and one draw needn't show every extreme that they name: `expert_ids`: each row names 8 different experts. Within the 2 rows of one device no expert is named more than 2 times, a bound that some block reaches on some device in every draw.
All inputs are finite; a program needn't handle non-finite values.
Results may differ from a plain program's by a relative error of at most 0.015.
Values may be sent and summed in bfloat16 or wider, within the bound.
A program may use at most 128 MiB of HBM per device.

v0:
```python
import jax
import jax.numpy as jnp
from jax import lax
from jax.sharding import PartitionSpec as P


def local(tokens, expert_ids, gate_ints, w_gate, w_up, w_down):
    groups = lax.axis_size("grp")
    members = lax.axis_size("ep")
    tok_rows, width = tokens.shape
    picks = expert_ids.shape[1]
    capacity = min(tok_rows, max(2, 3 * tok_rows * picks // (2 * groups)))
    routes = expert_ids.reshape(-1)
    onehot = (routes[:, None] == jnp.arange(groups, dtype=jnp.int32)[None, :]).astype(jnp.int32)
    earlier = jnp.cumsum(onehot, axis=0) - onehot
    slots = jnp.sum(earlier * onehot, axis=1)
    position = routes * capacity + slots
    token_index = jnp.arange(tok_rows * picks, dtype=jnp.int32) // picks
    table = jnp.zeros((groups * capacity,), jnp.int32).at[position].set(token_index)
    filled = jnp.zeros((groups * capacity,), jnp.bfloat16).at[position].set(1.0)
    dispatch = (tokens[table] * filled[:, None]).reshape(groups, capacity, width)
    gate_w = w_gate[0]
    up_w = w_up[0]
    down_w = w_down[0]
    outgoing = jnp.broadcast_to(dispatch[:, None], (groups, members, capacity, width))
    outgoing = outgoing.reshape(groups * members, capacity, width)
    arrived = lax.all_to_all(outgoing, ("grp", "ep"), split_axis=0, concat_axis=0, tiled=True)
    slot_count = arrived.shape[1]
    rows = arrived.reshape(-1, width)
    gate = jnp.dot(rows, gate_w, preferred_element_type=jnp.float32)
    up = jnp.dot(rows, up_w, preferred_element_type=jnp.float32)
    hidden = (jax.nn.silu(gate) * up).astype(jnp.bfloat16)
    partial_value = jnp.dot(hidden, down_w, preferred_element_type=jnp.float32)
    partial_value = partial_value.reshape(groups * members, slot_count, width)
    returned = lax.all_to_all(
        partial_value.astype(jnp.bfloat16), ("grp", "ep"), split_axis=0, concat_axis=0, tiled=True
    ).astype(partial_value.dtype)
    returned = returned.reshape(groups, members, slot_count, width)
    expert_out = jnp.sum(returned, axis=1).astype(jnp.bfloat16)
    flat_out = expert_out.reshape(groups * capacity, width)
    picked = flat_out[position].astype(jnp.float32)
    scores = gate_ints.astype(jnp.float32)
    weight = scores / jnp.sum(scores, axis=1, keepdims=True)
    mixed = jnp.sum(picked.reshape(tok_rows, picks, width) * weight[:, :, None], axis=1)
    return mixed.astype(jnp.bfloat16)


def solution(mesh):
    in_specs = (
        P(("grp", "ep"), None),
        P(("grp", "ep"), None),
        P(("grp", "ep"), None),
        P("grp", None, "ep"),
        P("grp", None, "ep"),
        P("grp", "ep", None),
    )
    out_specs = P(("grp", "ep"), None)
    return jax.shard_map(local, mesh=mesh, in_specs=in_specs, out_specs=out_specs, check_vma=False)
```

profile of v0, /device:TPU:0, one launch (start us, length us, event | category | flops | bytes accessed | tf_op | source)
XLA Modules:
  0.0 89.6 jit_solution(2443993452273369825)
XLA Ops:
  0.0 0.0 copy-start
  0.0 0.8 eq.15
  0.8 0.7 broadcast_multiply_fusion.1
  1.5 0.1 fusion.17
  1.6 0.2 select_reduce_fusion
  1.7 0.1 mul.46
  1.8 0.6 scatter_custom_fusion
  2.5 0.0 copy-done
  2.5 0.8 gather_fusion
  3.3 0.2 gather.9
  3.5 0.7 scatter_custom_fusion.1
  4.2 0.1 mul.48
  4.3 0.0 slice-start
  4.3 0.5 broadcast_multiply_fusion
  4.8 0.5 broadcast_in_dim.8
  5.2 30.6 %all_to_all.10 = bf16[32,2,7168]{2,1,0:T(2,128)(2,1)} all-to-all(bf16[32,2,7168]{2,1,0:T(2,128)(2,1)S(1)} %bitcast.32), channel_id=1, replica_groups=mesh['grp'=16,'ep'=2] {'grp','ep'}, dimensions={0} | all-to-all | bytes 1835008 | tf_op jit(solution)/shard_map/all_to_all | solution.py:27
  35.9 2.5 %reshape.67 = bf16[64,7168]{1,0:T(8,128)(2,1)S(1)} reshape(bf16[32,2,7168]{2,1,0:T(2,128)(2,1)} %all_to_all.10) | data formatting | bytes 1835008 | tf_op jit(solution)/shard_map/reshape | solution.py:29
  38.4 0.0 slice-start.1
  38.4 0.0 slice-start.2
  38.4 0.0 slice-start.3
  38.4 8.0 %fusion.4 = f32[64,1024]{1,0:T(8,128)S(1)} fusion(bf16[64,7168]{1,0:T(8,128)(2,1)S(1)} %reshape.67, bf16[1,7168,1024]{2,1,0:T(8,128)(2,1)} %param.9), kind=kOutput, calls=%fused_computation.8 | convolution fusion | flops 939524096 | bytes 15859712 | tf_op jit(solution)/shard_map/dot_general | solution.py:30
  46.4 0.0 slice-done
  46.4 0.0 slice-done.1
  46.4 0.0 slice-done.2
  46.4 0.8 slice-done.3
  47.2 2.7 %fusion.12 = bf16[64,1024]{1,0:T(8,128)(2,1)S(1)} fusion(bf16[64,7168]{1,0:T(8,128)(2,1)S(1)} %reshape.67, bf16[1,7168,1024]{2,1,0:T(8,128)(2,1)S(1)} %bitcast.31, f32[64,1024]{1,0:T(8,128)S(1)} %fusion.4), kind=kOutput, calls=%fused_computation.12 | convolution fusion | flops 939917312 | bytes 15990784 | tf_op jit(solution)/shard_map/dot_general | solution.py:31
  49.9 0.0 copy-start.1
  49.9 0.1 dot_general.13
  50.0 7.8 %fusion.6 = bf16[32,2,7168]{2,0,1:T(8,128)(2,1)S(1)} fusion(bf16[1,1024,7168]{2,1,0:T(8,128)(2,1)} %param.11, bf16[32,2,1024]{2,1,0:T(2,128)(2,1)S(1)} %dot_general.13), kind=kOutput, calls=%fused_computation.10 | convolution fusion | flops 939982848 | bytes 15728640 | tf_op jit(solution)/shard_map/dot_general | solution.py:33
  57.8 1.9 %copy.10 = bf16[32,2,7168]{2,1,0:T(2,128)(2,1)} copy(bf16[32,2,7168]{2,0,1:T(8,128)(2,1)S(1)} %fusion.6) | data formatting | bytes 1835008 | tf_op jit(solution)/shard_map/convert_element_type | solution.py:36
  59.7 3.6 %all-to-all-start.1 = ((bf16[32,2,7168]{2,1,0:T(2,128)(2,1)}), bf16[32,2,7168]{2,1,0:T(2,128)(2,1)S(1)}, u32[]{:S(2)}, u32[]{:S(2)}) async-start(bf16[32,2,7168]{2,1,0:T(2,128)(2,1)} %copy.10), calls=%async_computation.1 | async-start | bytes 1835008 | tf_op jit(solution)/shard_map/all_to_all | solution.py:35
  63.3 0.0 copy-done.1
  63.3 0.1 convert_reduce_fusion
  63.4 0.1 convert_divide_fusion
  63.5 23.2 %all-to-all-done.1 = bf16[32,2,7168]{2,1,0:T(2,128)(2,1)S(1)} async-done(((bf16[32,2,7168]{2,1,0:T(2,128)(2,1)}), bf16[32,2,7168]{2,1,0:T(2,128)(2,1)S(1)}, u32[]{:S(2)}, u32[]{:S(2)}) %all-to-all-start.1) | async-done | bytes 917536 | tf_op jit(solution)/shard_map/all_to_all | solution.py:35
  86.7 1.1 %bitcast_reduce_fusion = bf16[16,2,7168]{2,1,0:T(2,128)(2,1)S(1)} fusion(bf16[32,2,7168]{2,1,0:T(2,128)(2,1)S(1)} %all-to-all-done.1), kind=kLoop, calls=%fused_computation.13 | loop fusion | flops 229376 | bytes 1376256 | tf_op jit(solution)/shard_map/reduce_sum | solution.py:39
  87.8 0.2 convert_element_type.34
  88.0 0.7 gather_fusion.1
  88.7 0.9 fusion.15
  (8 shorter events, 0.1 us)
Async XLA Ops:
  0.0 2.5 %copy-start = (bf16[2,7168]{1,0:T(2,128)(2,1)S(1)}, bf16[2,7168]{1,0:T(2,128)(2,1)}, u32[]{:S(2)}) copy-start(bf16[2,7168]{1,0:T(2,128)(2,1)} %param.6) | copy-start | bytes 86020
  4.3 42.1 %slice-start = ((s8[14680064]{0:T(1024)(128)(4,1)}), s8[2097152]{0:T(1024)(128)(4,1)S(1)}, s32[]{:S(2)}) async-start(s8[14680064]{0:T(1024)(128)(4,1)} %bitcast.30), calls=%async_computation.2 | async-start | bytes 4194304
  38.4 8.1 %slice-start.1 = ((s8[14680064]{0:T(1024)(128)(4,1)}), s8[4194304]{0:T(1024)(128)(4,1)S(1)}, s32[]{:S(2)}) async-start(s8[14680064]{0:T(1024)(128)(4,1)} %bitcast.30), calls=%async_computation.3 | async-start | bytes 8388608
  38.4 8.1 %slice-start.2 = ((s8[14680064]{0:T(1024)(128)(4,1)}), s8[4194304]{0:T(1024)(128)(4,1)S(1)}, s32[]{:S(2)}) async-start(s8[14680064]{0:T(1024)(128)(4,1)} %bitcast.30), calls=%async_computation.4 | async-start | bytes 8388608
  38.4 8.8 %slice-start.3 = ((s8[14680064]{0:T(1024)(128)(4,1)}), s8[4194304]{0:T(1024)(128)(4,1)S(1)}, s32[]{:S(2)}) async-start(s8[14680064]{0:T(1024)(128)(4,1)} %bitcast.30), calls=%async_computation.5 | async-start | bytes 8388608
  49.9 13.4 %copy-start.1 = (s32[2,8]{1,0:T(2,128)S(1)}, s32[2,8]{1,0:T(2,128)}, u32[]{:S(2)}) copy-start(s32[2,8]{1,0:T(2,128)} %param.8) | copy-start | bytes 196
  59.7 27.0 %all-to-all-start.1 = ((bf16[32,2,7168]{2,1,0:T(2,128)(2,1)}), bf16[32,2,7168]{2,1,0:T(2,128)(2,1)S(1)}, u32[]{:S(2)}, u32[]{:S(2)}) async-start(bf16[32,2,7168]{2,1,0:T(2,128)(2,1)} %copy.10), calls=%async_computation.1 | async-start | bytes 1835008 | tf_op jit(solution)/shard_map/all_to_all | solution.py:35
where the time goes:
time: 89.9 us; the launch traced here: 89.6 us
  blocking collectives  30.6 us (34%)
  waiting for transfers between devices  23.2 us (26%)
  matrix products  18.5 us (21%)
  local copies, waits for them, and re-layouts  9.74 us (11%)
  other arithmetic  3.65 us (4%)
  starting transfers between devices  3.62 us (4%)
    all_to_all x1, blocking collectives, local(): lax.all_to_all(outgoing, ('grp', 'ep'), split_axis=0, concat_axis=0, tile...  30.6 us
    all_to_all x1, waiting for transfers between devices, local(): lax.all_to_all(partial_value.astype(jnp.bfloat16), ('grp', 'ep'), split_a...  23.2 us
    dot_general x1, matrix products, local(): gate = jnp.dot(rows, gate_w, preferred_element_type=jnp.float32)  8.01 us
    dot_general x1, matrix products, local(): partial_value = jnp.dot(hidden, down_w, preferred_element_type=jnp.float32)  7.83 us
    all_to_all x1, starting transfers between devices, local(): lax.all_to_all(partial_value.astype(jnp.bfloat16), ('grp', 'ep'), split_a...  3.62 us
    dot_general x1, matrix products, local(): up = jnp.dot(rows, up_w, preferred_element_type=jnp.float32)  2.71 us
    reshape x1, local copies, waits for them, and re-layouts, local(): rows = arrived.reshape(-1, width)  2.47 us
    convert_element_type x1, local copies, waits for them, and re-layouts, local(): partial_value.astype(jnp.bfloat16)  1.87 us
  transfers between devices with their start and end apart: 1, of which 1 were waited for; matrix products, arithmetic and copies ran while one was open for 0% of the time, Pallas kernels for 0%

commit v1 on v0

v1 whole, which is shorter than its diff:
```python
import functools
import jax
import jax.numpy as jnp
from jax import lax
from jax.experimental import pallas as pl
from jax.experimental.pallas import tpu as pltpu
from jax.sharding import PartitionSpec as P

MESH = pl.DeviceIdType.MESH
LANES = 128


def radices_of(count):
    found = []
    rest = count
    if rest % 2 == 0:
        found.append(2)
        rest //= 2
    while rest > 1:
        step = 4 if rest % 4 == 0 else (2 if rest % 2 == 0 else rest)
        found.append(step)
        rest //= step
    return found


def pieces_of(width, most):
    for count in range(most, 0, -1):
        if width % (count * 256) == 0:
            return count
    return 1


def kernel(cfg, tok_ref, ids_ref, gates_ref, wg_hbm, wu_hbm, wd_hbm, out_ref,
           zone, rows, wg, wu, wd, acc_g, acc_u, hid, share, *rest):
    radices, members, chunks, parts = cfg
    stages = len(radices)
    last = stages - 1
    sums = rest[:last]
    sends = rest[last:2 * last]
    recvs = rest[2 * last:3 * last]
    zsum, zsend, zrecv, wsem, gs, gr, rs, rr = rest[3 * last:]
    tok, width = tok_ref.shape
    kc = width // chunks
    nc = width // parts
    me = lax.axis_index("grp") * members + lax.axis_index("ep")
    strides, at = [], 1
    for radix in radices:
        strides.append(at)
        at *= radix
    digit = [lax.rem(lax.div(me, strides[i]), radices[i]) for i in range(stages)]
    span = [1] * last
    for i in range(last - 2, -1, -1):
        span[i] = span[i + 1] * radices[i + 1]

    def other(i, j):
        there = lax.rem(digit[i] + j, radices[i])
        flat = me + (there - digit[i]) * strides[i]
        return there, (lax.div(flat, members), lax.rem(flat, members))

    loads = []
    for c in range(chunks):
        at_k = pl.ds(c * kc, kc)
        loads.append(pltpu.make_async_copy(wg_hbm.at[0, at_k], wg.at[at_k], wsem.at[0, c]))
        loads.append(pltpu.make_async_copy(wu_hbm.at[0, at_k], wu.at[at_k], wsem.at[1, c]))
    downs = []
    for c in range(parts):
        at_n = pl.ds(c * nc, nc)
        downs.append(pltpu.make_async_copy(wd_hbm.at[0, :, at_n], wd.at[:, at_n], wsem.at[2, c]))
    for copy in loads + downs:
        copy.start()

    barrier = pltpu.get_barrier_semaphore()
    peers = 0
    for i in range(stages):
        for j in range(1, radices[i]):
            pl.semaphore_signal(barrier, inc=1, device_id=other(i, j)[1], device_id_type=MESH)
            peers += 1

    lane = lax.broadcasted_iota(jnp.int32, (tok, LANES), 1)
    ids = ids_ref[...]
    scores = gates_ref[...]
    dense = jnp.zeros((tok, LANES), jnp.int32)
    for k in range(ids.shape[1]):
        dense = dense + jnp.where(ids[:, k:k + 1] == lane, scores[:, k:k + 1], 0)
    zone[digit[last], :, pl.ds(0, width)] = tok_ref[...]
    zone[digit[last], :, pl.ds(width, LANES)] = dense.astype(jnp.float32).astype(jnp.bfloat16)
    pl.semaphore_wait(barrier, peers)

    def cols(c):
        return pl.ds(c * kc, kc + (LANES if c == chunks - 1 else 0))

    pending = []

    def push(src, dst, ssem, rsem, dev):
        copy = pltpu.make_async_remote_copy(
            src_ref=src, dst_ref=dst, send_sem=ssem, recv_sem=rsem, device_id=dev, device_id_type=MESH)
        copy.start()
        pending.append(copy)
        return copy

    flight = {}

    def gather_first(c):
        mine = zone.at[digit[last], :, cols(c)]
        flight["g", last, c] = [
            push(mine, mine, gs.at[last, c, j - 1], gr.at[last, c, j - 1], other(last, j)[1])
            for j in range(1, radices[last])]

    def unit_base(i):
        return sum(digit[k] * span[k] for k in range(i + 1))

    def gather_next(c, i):
        for copy in flight["g", i + 1, c]:
            copy.wait_recv()
        if i + 1 == last:
            got = [zone[d, :, cols(c)].astype(jnp.float32) for d in range(radices[last])]
            rows[unit_base(last - 1), :, cols(c)] = jnp.concatenate(got, axis=0).astype(jnp.bfloat16)
        if i >= 0:
            mine = rows.at[pl.ds(unit_base(i), span[i]), :, cols(c)]
            flight["g", i, c] = [
                push(mine, mine, gs.at[i, c, j - 1], gr.at[i, c, j - 1], other(i, j)[1])
                for j in range(1, radices[i])]

    units, unit_rows = rows.shape[0], rows.shape[1]
    total = units * unit_rows

    def up_chunk(c):
        at_k = pl.ds(c * kc, kc)
        loads[2 * c].wait()
        loads[2 * c + 1].wait()
        x = rows[:, :, at_k].astype(jnp.float32).reshape(total, kc).astype(jnp.bfloat16)
        g = jnp.dot(x, wg[at_k, :], preferred_element_type=jnp.float32)
        u = jnp.dot(x, wu[at_k, :], preferred_element_type=jnp.float32)
        if c == 0:
            acc_g[...] = g
            acc_u[...] = u
        else:
            acc_g[...] += g
            acc_u[...] += u

    for c in range(chunks):
        gather_first(c)
    for step in range(chunks + last):
        for i in range(last - 1, -2, -1):
            c = step - (last - 1 - i)
            if 0 <= c < chunks:
                gather_next(c, i)
                if i == -1:
                    up_chunk(c)

    expert = lax.axis_index("grp")
    meta = rows[:, :, pl.ds(width, LANES)].astype(jnp.float32).reshape(total, LANES)
    lanes = lax.broadcasted_iota(jnp.int32, (total, LANES), 1)
    chosen = jnp.sum(jnp.where(lanes == expert, meta, 0.0), axis=1, keepdims=True)
    weight = chosen / jnp.sum(meta, axis=1, keepdims=True)
    share[...] = jnp.broadcast_to(weight, share.shape)
    g = acc_g[...]
    hid[...] = (g / (1.0 + jnp.exp(-g)) * acc_u[...]).astype(jnp.bfloat16)

    def scatter_stage(i, c, value):
        at_n = pl.ds(c * nc, nc)
        value = value.reshape(radices[i], span[i], unit_rows, nc)
        sums[i][c] = value
        sends[i][:, :, :, at_n] = value.astype(jnp.bfloat16)
        copies = []
        for j in range(1, radices[i]):
            there, dev = other(i, j)
            copies.append(push(sends[i].at[there, :, :, at_n], recvs[i].at[j - 1, :, :, at_n],
                               rs.at[i, c, j - 1], rr.at[i, c, j - 1], dev))
        flight["s", i, c] = copies

    def scatter_last(c, value):
        at_n = pl.ds(c * nc, nc)
        value = value.reshape(unit_rows, nc)
        for d in range(radices[last]):
            one = value[d * tok:(d + 1) * tok, :]
            zsum[c, d] = one
            zsend[d, :, at_n] = one.astype(jnp.bfloat16)
        copies = []
        for j in range(1, radices[last]):
            there, dev = other(last, j)
            copies.append(push(zsend.at[there, :, at_n], zrecv.at[j - 1, :, at_n],
                               rs.at[last, c, j - 1], rr.at[last, c, j - 1], dev))
        flight["s", last, c] = copies

    def scatter_step(c, i):
        at_n = pl.ds(c * nc, nc)
        if i == -1:
            downs[c].wait()
            part = jnp.dot(hid[...], wd[:, at_n], preferred_element_type=jnp.float32)
            part = part * share[:, :1]
            scatter_stage(0, c, part)
            return
        for copy in flight["s", i, c]:
            copy.wait_recv()
        if i == last:
            value = zsum[c, digit[last]]
            for j in range(radices[last] - 1):
                value = value + zrecv[j, :, at_n].astype(jnp.float32)
            out_ref[:, at_n] = value.astype(jnp.bfloat16)
            return
        value = sums[i][c, digit[i]]
        for j in range(radices[i] - 1):
            value = value + recvs[i][j, :, :, at_n].astype(jnp.float32)
        if i + 1 == last:
            scatter_last(c, value)
        else:
            scatter_stage(i + 1, c, value)

    for step in range(parts + stages):
        for i in range(-1, stages):
            c = step - (i + 1)
            if 0 <= c < parts:
                scatter_step(c, i)
    for copy in pending:
        copy.wait_send()


def local(cfg, tokens, expert_ids, gate_ints, w_gate, w_up, w_down):
    radices, members, chunks, parts = cfg
    stages = len(radices)
    last = stages - 1
    tok, width = tokens.shape
    hidden = w_gate.shape[2]
    count = 1
    for radix in radices:
        count *= radix
    units = count // radices[last]
    unit_rows = radices[last] * tok
    total = units * unit_rows
    nc = width // parts
    most = max(radices) - 1
    span = [1] * last
    for i in range(last - 2, -1, -1):
        span[i] = span[i + 1] * radices[i + 1]
    bf, f32 = jnp.bfloat16, jnp.float32
    scratch = [
        pltpu.VMEM((radices[last], tok, width + LANES), bf),
        pltpu.VMEM((units, unit_rows, width + LANES), bf),
        pltpu.VMEM((width, hidden), bf),
        pltpu.VMEM((width, hidden), bf),
        pltpu.VMEM((hidden, width), bf),
        pltpu.VMEM((total, hidden), f32),
        pltpu.VMEM((total, hidden), f32),
        pltpu.VMEM((total, hidden), bf),
        pltpu.VMEM((total, LANES), f32),
    ]
    scratch += [pltpu.VMEM((parts, radices[i], span[i], unit_rows, nc), f32) for i in range(last)]
    scratch += [pltpu.VMEM((radices[i], span[i], unit_rows, width), bf) for i in range(last)]
    scratch += [pltpu.VMEM((radices[i] - 1, span[i], unit_rows, width), bf) for i in range(last)]
    scratch += [
        pltpu.VMEM((parts, radices[last], tok, nc), f32),
        pltpu.VMEM((radices[last], tok, width), bf),
        pltpu.VMEM((radices[last] - 1, tok, width), bf),
        pltpu.SemaphoreType.DMA((3, max(chunks, parts))),
        pltpu.SemaphoreType.DMA((stages, chunks, most)),
        pltpu.SemaphoreType.DMA((stages, chunks, most)),
        pltpu.SemaphoreType.DMA((stages, parts, most)),
        pltpu.SemaphoreType.DMA((stages, parts, most)),
    ]
    vmem = pl.BlockSpec(memory_space=pltpu.VMEM)
    hbm = pl.BlockSpec(memory_space=pl.ANY)
    return pl.pallas_call(
        functools.partial(kernel, cfg),
        out_shape=jax.ShapeDtypeStruct((tok, width), bf),
        in_specs=[vmem, vmem, vmem, hbm, hbm, hbm],
        out_specs=vmem,
        scratch_shapes=scratch,
        compiler_params=pltpu.CompilerParams(
            collective_id=0, has_side_effects=True, vmem_limit_bytes=62 * 1024 * 1024),
    )(tokens, expert_ids, gate_ints, w_gate, w_up, w_down)


def solution(mesh):
    count = mesh.shape["grp"] * mesh.shape["ep"]

    def step(tokens, expert_ids, gate_ints, w_gate, w_up, w_down):
        width = tokens.shape[1]
        cfg = (tuple(radices_of(count)), mesh.shape["ep"], pieces_of(width, 4), pieces_of(width, 4))
        return local(cfg, tokens, expert_ids, gate_ints, w_gate, w_up, w_down)

    in_specs = (
        P(("grp", "ep"), None),
        P(("grp", "ep"), None),
        P(("grp", "ep"), None),
        P("grp", None, "ep"),
        P("grp", None, "ep"),
        P("grp", "ep", None),
    )
    out_specs = P(("grp", "ep"), None)
    return jax.shard_map(step, mesh=mesh, in_specs=in_specs, out_specs=out_specs, check_vma=False)
```

time: 89.9 us -> 42.8 us (0.48)
  Pallas kernels: 0 us -> 41.2 us
  blocking collectives: 30.6 us -> 0 us
  waiting for transfers between devices: 23.2 us -> 0 us
  matrix products: 18.5 us -> 0 us
  local copies, waits for them, and re-layouts: 9.74 us -> 1.38 us
  other arithmetic: 3.65 us -> 0 us
  starting transfers between devices: 3.62 us -> 0 us
    pallas_call x0 -> x1, Pallas kernels: none -> 41.2 us  [local(): pl.pallas_call(functools.partial(kernel, cfg), out_shape=jax.ShapeDtypeSt...]
    all_to_all x1 -> x0, blocking collectives: 30.6 us -> none  [local(): lax.all_to_all(outgoing, ('grp', 'ep'), split_axis=0, concat_axis=0, tile...]
    all_to_all x1 -> x0, waiting for transfers between devices: 23.2 us -> none  [local(): lax.all_to_all(partial_value.astype(jnp.bfloat16), ('grp', 'ep'), split_a...]
    dot_general x3 -> x0, matrix products: 18.5 us -> none  [the longest x1 8.01 us: local(): gate = jnp.dot(rows, gate_w, preferred_element_type=jnp.float32)]
    all_to_all x1 -> x0, starting transfers between devices: 3.62 us -> none  [local(): lax.all_to_all(partial_value.astype(jnp.bfloat16), ('grp', 'ep'), split_a...]
    reshape x1 -> x0, local copies, waits for them, and re-layouts: 2.47 us -> none  [local(): rows = arrived.reshape(-1, width)]
    reduce_sum x4 -> x0, other arithmetic: 2.29 us -> none  [the longest x1 1.12 us: local(): expert_out = jnp.sum(returned, axis=1).astype(jnp.bfloat16)]
    convert_element_type x2 -> x0, local copies, waits for them, and re-layouts: 2.05 us -> none  [the longest x1 1.87 us: local(): partial_value.astype(jnp.bfloat16)]
  transfers between devices with their start and end apart: 1 -> 0, of which waited for: 1 -> 0; matrix products, arithmetic and copies ran while one was open for 0% -> 0% of each run, Pallas kernels for 0% -> 0%
where the time goes in v1:
time: 42.8 us; the launch traced here: 42.6 us
  Pallas kernels  41.2 us (96%)
  local copies, waits for them, and re-layouts  1.38 us (3%)
    pallas_call x1, Pallas kernels, local(): pl.pallas_call(functools.partial(kernel, cfg), out_shape=jax.ShapeDtypeSt...  41.2 us
    unnamed x1, local copies, waits for them, and re-layouts  1.38 us

profile of v1, /device:TPU:0, one launch (start us, length us, event | category | flops | bytes accessed | tf_op | source)
XLA Modules:
  0.0 42.6 jit_solution(7270338953988877458)
XLA Ops:
  0.0 41.2 %shard_map.64 = bf16[2,7168]{1,0:T(2,128)(2,1)} custom-call(bf16[2,7168]{1,0:T(2,128)(2,1)} %tok_ref.1, s32[2,8]{1,0:T(2,128)} %ids_ref.1, s32[2,8]{1,0:T(2,128)} %gates_ref.1, bf16[1,7168,1024]{2,1,0:T(8,128)(2,1)} %wg_hbm.1, bf16[1,7168,1024]{2,1,0:T(8,128)(2,1)} %wu_hbm.1, bf16[1,1024,7168]{2,1,0:T(8,128)(2,1)} %wd_hbm.1), custom_call_target="tpu_custom_call" | custom-call | tf_op jit(solution)/shard_map/pallas_call | solution.py:263
  41.2 1.4 %copy.8 = bf16[2,7168]{1,0:T(2,128)(2,1)} copy(bf16[2,7168]{1,0:T(2,128)(2,1)} %shard_map.64) | data formatting | bytes 57344

commit v2 on v1

--- a/solution.py
+++ b/solution.py
@@ -276,7 +276,7 @@
 
     def step(tokens, expert_ids, gate_ints, w_gate, w_up, w_down):
         width = tokens.shape[1]
-        cfg = (tuple(radices_of(count)), mesh.shape["ep"], pieces_of(width, 4), pieces_of(width, 4))
+        cfg = (tuple(radices_of(count)), mesh.shape["ep"], pieces_of(width, 2), pieces_of(width, 2))
         return local(cfg, tokens, expert_ids, gate_ints, w_gate, w_up, w_down)
 
     in_specs = (

time: 42.8 us -> 38.1 us (0.89)
  Pallas kernels: 41.2 us -> 36.5 us
    pallas_call x1, Pallas kernels: 41.2 us -> 36.5 us  [local(): pl.pallas_call(functools.partial(kernel, cfg), out_shape=jax.ShapeDtypeSt...]
where the time goes in v2:
time: 38.1 us; the launch traced here: 37.9 us
  Pallas kernels  36.5 us (96%)
  local copies, waits for them, and re-layouts  1.38 us (4%)
    pallas_call x1, Pallas kernels, local(): pl.pallas_call(functools.partial(kernel, cfg), out_shape=jax.ShapeDtypeSt...  36.5 us
    unnamed x1, local copies, waits for them, and re-layouts  1.38 us

profile of v2, /device:TPU:0, one launch (start us, length us, event | category | flops | bytes accessed | tf_op | source)
XLA Modules:
  0.0 37.9 jit_solution(12513930227991235781)
XLA Ops:
  0.0 36.5 %shard_map.64 = bf16[2,7168]{1,0:T(2,128)(2,1)} custom-call(bf16[2,7168]{1,0:T(2,128)(2,1)} %tok_ref.1, s32[2,8]{1,0:T(2,128)} %ids_ref.1, s32[2,8]{1,0:T(2,128)} %gates_ref.1, bf16[1,7168,1024]{2,1,0:T(8,128)(2,1)} %wg_hbm.1, bf16[1,7168,1024]{2,1,0:T(8,128)(2,1)} %wu_hbm.1, bf16[1,1024,7168]{2,1,0:T(8,128)(2,1)} %wd_hbm.1), custom_call_target="tpu_custom_call" | custom-call | tf_op jit(solution)/shard_map/pallas_call | solution.py:263
  36.5 1.4 %copy.8 = bf16[2,7168]{1,0:T(2,128)(2,1)} copy(bf16[2,7168]{1,0:T(2,128)(2,1)} %shard_map.64) | data formatting | bytes 57344

commit v3 on v2

--- a/solution.py
+++ b/solution.py
@@ -104,7 +104,7 @@
         mine = zone.at[digit[last], :, cols(c)]
         flight["g", last, c] = [
             push(mine, mine, gs.at[last, c, j - 1], gr.at[last, c, j - 1], other(last, j)[1])
-            for j in range(1, radices[last])]
+            for j in sorted(range(1, radices[last]), key=lambda j: abs(j - 2))]
 
     def unit_base(i):
         return sum(digit[k] * span[k] for k in range(i + 1))
@@ -119,7 +119,7 @@
             mine = rows.at[pl.ds(unit_base(i), span[i]), :, cols(c)]
             flight["g", i, c] = [
                 push(mine, mine, gs.at[i, c, j - 1], gr.at[i, c, j - 1], other(i, j)[1])
-                for j in range(1, radices[i])]
+                for j in sorted(range(1, radices[i]), key=lambda j: abs(j - 2))]
 
     units, unit_rows = rows.shape[0], rows.shape[1]
     total = units * unit_rows
@@ -163,7 +163,7 @@
         sums[i][c] = value
         sends[i][:, :, :, at_n] = value.astype(jnp.bfloat16)
         copies = []
-        for j in range(1, radices[i]):
+        for j in sorted(range(1, radices[i]), key=lambda j: abs(j - 2)):
             there, dev = other(i, j)
             copies.append(push(sends[i].at[there, :, :, at_n], recvs[i].at[j - 1, :, :, at_n],
                                rs.at[i, c, j - 1], rr.at[i, c, j - 1], dev))

time: 38.1 us -> 38.2 us (level)
  no operation moved by 1% of the time
where the time goes in v3:
time: 38.2 us; the launch traced here: 37.9 us
  Pallas kernels  36.5 us (96%)
  local copies, waits for them, and re-layouts  1.38 us (4%)
    pallas_call x1, Pallas kernels, local(): pl.pallas_call(functools.partial(kernel, cfg), out_shape=jax.ShapeDtypeSt...  36.5 us
    unnamed x1, local copies, waits for them, and re-layouts  1.38 us

profile of v3, /device:TPU:0, one launch (start us, length us, event | category | flops | bytes accessed | tf_op | source)
XLA Modules:
  0.0 37.9 jit_solution(9506069705558914096)
XLA Ops:
  0.0 36.5 %shard_map.64 = bf16[2,7168]{1,0:T(2,128)(2,1)} custom-call(bf16[2,7168]{1,0:T(2,128)(2,1)} %tok_ref.1, s32[2,8]{1,0:T(2,128)} %ids_ref.1, s32[2,8]{1,0:T(2,128)} %gates_ref.1, bf16[1,7168,1024]{2,1,0:T(8,128)(2,1)} %wg_hbm.1, bf16[1,7168,1024]{2,1,0:T(8,128)(2,1)} %wu_hbm.1, bf16[1,1024,7168]{2,1,0:T(8,128)(2,1)} %wd_hbm.1), custom_call_target="tpu_custom_call" | custom-call | tf_op jit(solution)/shard_map/pallas_call | solution.py:263
  36.5 1.4 %copy.8 = bf16[2,7168]{1,0:T(2,128)(2,1)} copy(bf16[2,7168]{1,0:T(2,128)(2,1)} %shard_map.64) | data formatting | bytes 57344
